TPU v7x, 32 devices: a whole 2x2x4 slice. The times are simulated.
32 devices in a mesh: group: 2 (over y), head: 4 (over z), cache: 4 (over x, core).
Axes of the slice: x: 2, y: 2, z: 4, core: 2. Of those that a mesh axis runs over, the one named last changes fastest.
Arguments:
- queries: bfloat16 [512, 4096], P(('group', 'head')), parts along dimension 0, may hold values from -8 to 8
- keys: bfloat16 [256, 128, 4096], P(('group', 'cache'), None, 'head'), parts along dimension 0, may hold values from -8 to 8
- values: bfloat16 [256, 128, 4096], P(('group', 'cache'), None, 'head'), parts along dimension 0, may hold values from -6 to 6
- page_lists: int32 [8, 32], P(('group', 'cache')), parts along dimension 0, may hold values from 0 to 31, as said below
- page_counts: int32 [8], P(('group', 'cache')), parts along dimension 0, may hold values from 1 to 32, as said below
Outputs:
- attended: float32 [512, 4096], P(('group', 'head', 'cache')), parts along dimension 0
- log_sums: float32 [512, 32], P(('group', 'head', 'cache')), parts along dimension 0
There are 2 independent parts, one for each index of `group`. A program takes and returns all parts, laid end to end along the dimension named above; each array names one. Nothing has to cross between parts.
Inputs may be any that keep to these rules, and one draw needn't show every extreme that they name: `page_lists`: row c holds 32 distinct page ids of owner c's pool; only its first page_counts[c] entries are attended. `page_counts`: some owner lists exactly 32 pages in every draw.
All inputs are finite; a program needn't handle non-finite values.
Results may differ from a plain program's by a relative error of at most 0.00038.
Values may be sent and summed in bfloat16 or wider, within the bound.
A program may use at most 64 MiB of HBM per device.

v0:
```python
import math

import jax
import jax.numpy as jnp
from jax import lax
from jax.sharding import PartitionSpec as P

HEADS = 32
DH = 128
PAGE = 128


lowest = -1e30


def combined_all(value, axis, join):
    pieces = jax.tree.map(lambda part: lax.all_gather(part, axis), value)
    head = jax.tree.map(lambda part: part[0], pieces)
    tail = jax.tree.map(lambda part: part[1:], pieces)
    so_far, _ = lax.scan(lambda so_far, share: (join(so_far, share), None), head, tail)
    return so_far


def join_states(first, second):
    best_first, total_first, accum_first = first
    best_second, total_second, accum_second = second
    top = jnp.maximum(best_first, best_second)
    keep_first = jnp.exp(best_first - top)
    keep_second = jnp.exp(best_second - top)
    total = total_first * keep_first + total_second * keep_second
    accum = accum_first * keep_first[..., None] + accum_second * keep_second[..., None]
    return (top, total, accum)


def on_device(queries, keys, values, page_lists, page_counts):
    n_head = lax.axis_size("head")
    n_cache = lax.axis_size("cache")
    tok_local = queries.shape[0]
    local_heads = keys.shape[2] // DH
    all_tok = tok_local * n_head
    share = all_tok // (n_head * n_cache)
    score_scale = 1.0 / math.sqrt(DH)
    moved = lax.all_to_all(
        queries.reshape(tok_local, n_head, local_heads * DH),
        "head",
        split_axis=1,
        concat_axis=0,
        tiled=True,
    )
    query_heads = moved.reshape(all_tok, local_heads, DH)
    pool_keys = keys.reshape(keys.shape[0], PAGE, local_heads, DH)
    pool_values = values.reshape(values.shape[0], PAGE, local_heads, DH)
    listed = page_lists[0]
    count = page_counts[0]
    blocks = (count + 3) // 4

    def visit_block(block, state):
        best, total, accum = state
        first = block * 4
        page_ids = lax.dynamic_slice_in_dim(listed, first, 4)
        usable = first + jnp.arange(4, dtype=jnp.int32) < count
        key_block = pool_keys[page_ids]
        value_block = pool_values[page_ids]
        scores = (
            jnp.einsum("thd,pkhd->thpk", query_heads, key_block, preferred_element_type=jnp.float32)
            * score_scale
        )
        page_max = jnp.max(scores, axis=-1)
        weights = jnp.exp(scores - page_max[..., None]).astype(jnp.bfloat16)
        page_sum = jnp.sum(weights, axis=-1, dtype=jnp.float32)
        page_out = jnp.einsum(
            "thpk,pkhd->thpd", weights, value_block, preferred_element_type=jnp.float32
        )
        used_max = jnp.where(usable[None, None, :], page_max, lowest)
        running = jnp.maximum(best, jnp.max(used_max, axis=-1))
        fresh = jnp.exp(used_max - running[..., None])
        keep = jnp.exp(best - running)
        total = total * keep + jnp.sum(fresh * page_sum, axis=-1)
        accum = accum * keep[..., None] + jnp.sum(fresh[..., None] * page_out, axis=2)
        return (running, total, accum)

    start = (
        jnp.full((all_tok, local_heads), lowest, jnp.float32),
        jnp.zeros((all_tok, local_heads), jnp.float32),
        jnp.zeros((all_tok, local_heads, DH), jnp.float32),
    )
    best, total, accum = lax.fori_loop(0, blocks, visit_block, start)
    position = lax.axis_index("cache")
    best, total, accum = combined_all((best, total, accum), "cache", join_states)
    result = accum / total[..., None]
    logged = best + jnp.log(total)
    result = lax.dynamic_index_in_dim(
        result.reshape(n_head, n_cache, share, local_heads, DH), position, 1, keepdims=False
    )
    logged = lax.dynamic_index_in_dim(
        logged.reshape(n_head, n_cache, share, local_heads), position, 1, keepdims=False
    )
    result, logged = (
        lax.all_to_all(result, "head", split_axis=0, concat_axis=2, tiled=True),
        lax.all_to_all(logged, "head", split_axis=0, concat_axis=2, tiled=True),
    )
    return (result.reshape(share, HEADS * DH), logged.reshape(share, HEADS))


def solution(mesh):
    in_specs = (
        P(("group", "head"), None),
        P(("group", "cache"), None, "head"),
        P(("group", "cache"), None, "head"),
        P(("group", "cache"), None),
        P(("group", "cache")),
    )
    out_specs = (P(("group", "head", "cache"), None), P(("group", "head", "cache"), None))
    return jax.shard_map(
        on_device, mesh=mesh, in_specs=in_specs, out_specs=out_specs, check_vma=False
    )
```

profile of v0, /device:TPU:0, one launch (start us, length us, event | category | flops | bytes accessed | tf_op | source)
XLA Modules:
  0.0 244.5 jit_solution(14165468163173509033)
XLA Ops:
  9.0 6.3 %all-to-all-start = ((bf16[64,4,1024]{2,0,1:T(8,128)(2,1)}), bf16[64,4,1024]{2,0,1:T(8,128)(2,1)S(1)}, u32[]{:S(2)}, u32[]{:S(2)}) async-start(bf16[64,4,1024]{2,0,1:T(8,128)(2,1)} %bitcast.86), calls=%async_computation | async-start | bytes 1048576 | tf_op jit(solution)/shard_map/all_to_all | solution.py:43
  16.0 8.8 %copy.57 = bf16[512,8,8,128]{3,2,1,0:T(8,128)(2,1)} copy(bf16[512,8,8,128]{3,1,2,0:T(8,128)(2,1)} %bitcast.107) | data formatting | bytes 16777216
  24.8 8.8 %copy.59 = bf16[512,8,8,128]{3,2,1,0:T(8,128)(2,1)} copy(bf16[512,8,8,128]{3,1,2,0:T(8,128)(2,1)} %bitcast.108) | data formatting | bytes 16777216
  33.9 33.4 %while.28 = (s32[]{:T(128)}, f32[256,8]{0,1:T(8,128)S(1)}, f32[256,8]{0,1:T(8,128)S(1)}, f32[256,8,128]{0,2,1:T(8,128)S(1)}, s32[]{:T(128)}, /*index=5*/s32[]{:T...) while((s32[]{:T(128)}, f32[256,8]{0,1:T(8,128)S(1)}, ...), condition=%wide.region_6.7_spmd, body=%wide.region_0.6_spmd.sunk | while | flops 549753856 | bytes 40792384 | solution.py:87
  34.0 4.1 %gather_fusion = bf16[4,128,8,128]{3,2,1,0:T(8,128)(2,1)S(1)} fusion(bf16[32,128,8,128]{3,2,1,0:T(8,128)(2,1)} %get-tuple-element.342, s32[1024]{0:T(1024)S(1)} %pad_clamp_fusion.2), kind=kCustom, calls=%fused_computation.clone.1 | custom fusion | bytes 2097168 | tf_op jit(solution)/shard_map/while/body/gather | solution.py:62
  38.9 1.9 copy-done
  42.6 4.1 %gather_fusion.1 = bf16[4,128,8,128]{3,2,1,0:T(8,128)(2,1)S(1)} fusion(bf16[32,128,8,128]{3,2,1,0:T(8,128)(2,1)} %get-tuple-element.344, s32[1024]{0:T(1024)S(1)} %pad_clamp_fusion.2), kind=kCustom, calls=%fused_computation.1.clone.1 | custom fusion | bytes 2097168 | tf_op jit(solution)/shard_map/while/body/gather | solution.py:63
  46.7 3.5 %fusion.21 = f32[256,8,128]{0,2,1:T(8,128)S(1)} fusion(f32[256,8,4]{0,2,1:T(4,128)S(1)} %get-tuple-element.294, bf16[4,128,8,128]{3,2,1,0:T(8,128)(2,1)S(1)} %gather_fusion.1, f32[8,4,128,256]{3,2,1,0:T(8,128)} %copy-done, f32[256,8,4]{0,2,1:T(4,128)S(1)} %get-tuple-element.290), kind=kOutput, calls=%fused_computation.11.clone.1 | convolution fusion | flops 273416192 | bytes 6356992 | tf_op jit(solution)/shard_map/while/body/thpk,pkhd->thpd/dot_general | solution.py:71
  50.7 4.1 %gather_fusion = bf16[4,128,8,128]{3,2,1,0:T(8,128)(2,1)S(1)} fusion(bf16[32,128,8,128]{3,2,1,0:T(8,128)(2,1)} %get-tuple-element.342, s32[1024]{0:T(1024)S(1)} %pad_clamp_fusion.2), kind=kCustom, calls=%fused_computation.clone.1 | custom fusion | bytes 2097168 | tf_op jit(solution)/shard_map/while/body/gather | solution.py:62
  55.6 1.9 copy-done
  59.3 4.1 %gather_fusion.1 = bf16[4,128,8,128]{3,2,1,0:T(8,128)(2,1)S(1)} fusion(bf16[32,128,8,128]{3,2,1,0:T(8,128)(2,1)} %get-tuple-element.344, s32[1024]{0:T(1024)S(1)} %pad_clamp_fusion.2), kind=kCustom, calls=%fused_computation.1.clone.1 | custom fusion | bytes 2097168 | tf_op jit(solution)/shard_map/while/body/gather | solution.py:63
  63.4 3.5 %fusion.21 = f32[256,8,128]{0,2,1:T(8,128)S(1)} fusion(f32[256,8,4]{0,2,1:T(4,128)S(1)} %get-tuple-element.294, bf16[4,128,8,128]{3,2,1,0:T(8,128)(2,1)S(1)} %gather_fusion.1, f32[8,4,128,256]{3,2,1,0:T(8,128)} %copy-done, f32[256,8,4]{0,2,1:T(4,128)S(1)} %get-tuple-element.290), kind=kOutput, calls=%fused_computation.11.clone.1 | convolution fusion | flops 273416192 | bytes 6356992 | tf_op jit(solution)/shard_map/while/body/thpk,pkhd->thpd/dot_general | solution.py:71
  68.6 104.4 %all-gather = f32[1024,8]{0,1:T(8,128)S(1)} all-gather(f32[256,8]{0,1:T(8,128)S(1)} %get-tuple-element.96), channel_id=2, replica_groups=mesh['group'=2,'head'=4,'cache'=4] {'cache'}, dimensions={0}, use_global_device_ids=true | all-gather | bytes 40960 | tf_op jit(solution)/shard_map/all_gather | solution.py:17
  173.0 5.2 %all-gather.1 = f32[1024,8]{0,1:T(8,128)S(1)} all-gather(f32[256,8]{0,1:T(8,128)S(1)} %get-tuple-element.97), channel_id=3, replica_groups=mesh['group'=2,'head'=4,'cache'=4] {'cache'}, dimensions={0}, use_global_device_ids=true | all-gather | bytes 40960 | tf_op jit(solution)/shard_map/all_gather | solution.py:17
  178.2 25.6 %all-gather.5.cloned.1.call-done = f32[1024,8,128]{2,1,0:T(8,128)} async-done(((f32[256,8,128]{2,1,0:T(8,128)}), f32[1024,8,128]{2,1,0:T(8,128)}) %all-gather.5.cloned.1.call-update) | async-done | bytes 4194320 | tf_op jit(solution)/shard_map/all_gather | solution.py:17
  203.8 3.9 %slice.39 = f32[768,8,128]{2,1,0:T(8,128)} slice(f32[1024,8,128]{2,1,0:T(8,128)} %all-gather.5.cloned.1.call-done), slice={[256:1024], [0:8], [0:128]} | slice | bytes 6291456 | tf_op jit(solution)/shard_map/slice | solution.py:19
  207.7 6.6 %while.29 = (s32[]{:T(128)}, f32[256,8]{0,1:T(8,128)S(1)}, f32[256,8]{0,1:T(8,128)S(1)}, f32[256,8,128]{2,1,0:T(8,128)S(1)}, f32[3,256,8]{1,2,0:T(8,128)S(1)}, /...) while((s32[]{:T(128)}, f32[256,8]{0,1:T(8,128)S(1)}, f32[256,8]{0,1:T(8,128)S(1)}, ...), condition=%wide.region_8.9_spmd, body=%wide.region_7.8_spmd.sunk | while | flops 798722 | bytes 3260517 | solution.py:20
  208.0 1.9 fusion.23
  210.2 1.9 fusion.23
  212.4 1.9 fusion.23
  215.2 4.6 %all-to-all-start.2 = ((f32[4,1,128]{2,1,0:T(1,128)}), f32[4,1,128]{2,1,0:T(1,128)S(1)}, u32[]{:S(2)}, u32[]{:S(2)}) async-start(f32[4,1,128]{2,1,0:T(1,128)} %reshape.86), calls=%async_computation.2 | async-start | bytes 4096 | tf_op jit(solution)/shard_map/all_to_all | solution.py:100
  220.9 4.4 %all-to-all-done.2 = f32[4,1,128]{2,1,0:T(1,128)S(1)} async-done(((f32[4,1,128]{2,1,0:T(1,128)}), f32[4,1,128]{2,1,0:T(1,128)S(1)}, u32[]{:S(2)}, u32[]{:S(2)}) %all-to-all-start.2) | async-done | bytes 2080 | tf_op jit(solution)/shard_map/all_to_all | solution.py:100
  225.3 3.4 %all-to-all-start.1 = ((f32[4,16,8,128]{3,2,1,0:T(8,128)}), f32[4,16,8,128]{3,2,1,0:T(8,128)S(1)}, u32[]{:S(2)}, u32[]{:S(2)}) async-start(f32[4,16,8,128]{3,2,1,0:T(8,128)} %dynamic-slice_bitcast_fusion), calls=%async_computation.1 | async-start | bytes 524288 | tf_op jit(solution)/shard_map/all_to_all | solution.py:99
  230.7 6.2 %all-to-all-done.1 = f32[4,16,8,128]{3,2,1,0:T(8,128)S(1)} async-done(((f32[4,16,8,128]{3,2,1,0:T(8,128)}), f32[4,16,8,128]{3,2,1,0:T(8,128)S(1)}, u32[]{:S(2)}, u32[]{:S(2)}) %all-to-all-start.1) | async-done | bytes 262176 | tf_op jit(solution)/shard_map/all_to_all | solution.py:99
  (66 shorter events, 14.8 us)
Async XLA Ops:
  9.0 24.6 %all-to-all-start = ((bf16[64,4,1024]{2,0,1:T(8,128)(2,1)}), bf16[64,4,1024]{2,0,1:T(8,128)(2,1)S(1)}, u32[]{:S(2)}, u32[]{:S(2)}) async-start(bf16[64,4,1024]{2,0,1:T(8,128)(2,1)} %bitcast.86), calls=%async_computation | async-start | bytes 1048576 | tf_op jit(solution)/shard_map/all_to_all | solution.py:43
  15.4 188.5 %all-gather.5.cloned.1.call-start = ((), (), s32[]{:S(2)}) async-start(), calls=%async_computation.3 | async-start | bytes 5242880 | tf_op jit(solution)/shard_map/all_gather | solution.py:17
  24.8 9.1 %copy-start.1 = (s32[1,32]{1,0:T(1,128)S(1)}, s32[1,32]{1,0:T(1,128)}, u32[]{:S(2)}) copy-start(s32[1,32]{1,0:T(1,128)} %param.12) | copy-start | bytes 388
  38.9 1.9 copy-start
  55.6 1.9 copy-start
  203.8 3.9 %slice-start = ((f32[1024,8,128]{2,1,0:T(8,128)}), f32[256,8,128]{2,1,0:T(8,128)S(1)}, s32[]{:S(2)}) async-start(f32[1024,8,128]{2,1,0:T(8,128)} %all-gather.5.cloned.1.call-done), calls=%async_computation.4 | async-start | bytes 2097152 | tf_op jit(solution)/shard_map/slice | solution.py:18
  215.2 10.1 %all-to-all-start.2 = ((f32[4,1,128]{2,1,0:T(1,128)}), f32[4,1,128]{2,1,0:T(1,128)S(1)}, u32[]{:S(2)}, u32[]{:S(2)}) async-start(f32[4,1,128]{2,1,0:T(1,128)} %reshape.86), calls=%async_computation.2 | async-start | bytes 4096 | tf_op jit(solution)/shard_map/all_to_all | solution.py:100
  225.3 11.6 %all-to-all-start.1 = ((f32[4,16,8,128]{3,2,1,0:T(8,128)}), f32[4,16,8,128]{3,2,1,0:T(8,128)S(1)}, u32[]{:S(2)}, u32[]{:S(2)}) async-start(f32[4,16,8,128]{3,2,1,0:T(8,128)} %dynamic-slice_bitcast_fusion), calls=%async_computation.1 | async-start | bytes 524288 | tf_op jit(solution)/shard_map/all_to_all | solution.py:99
Sparse Core Ops, SparseCore 0:
  68.7 135.0 all-gather.4
where the time goes:
time: 246 us; the launch traced here: 245 us
  blocking collectives  110 us (45%)
  local copies, waits for them, and re-layouts  49.7 us (20%)
  waiting for transfers between devices  36.3 us (15%)
  between operations  14.8 us (6%)
  starting transfers between devices  14.4 us (6%)
  other arithmetic  11.2 us (5%)
  matrix products  8.4 us (3%)
    all_gather x2, blocking collectives, combined_all(): pieces = jax.tree.map(lambda part: lax.all_gather(part, axis), value)  110 us
    all_gather x1, waiting for transfers between devices, combined_all(): pieces = jax.tree.map(lambda part: lax.all_gather(part, axis), value)  25.6 us
    unnamed x8, local copies, waits for them, and re-layouts  19.1 us
    gather x2, local copies, waits for them, and re-layouts, visit_block(): value_block = pool_values[page_ids]  8.26 us
    gather x2, local copies, waits for them, and re-layouts, visit_block(): key_block = pool_keys[page_ids]  8.26 us
    dot_general x2, matrix products, visit_block(): jnp.einsum('thpk,pkhd->thpd', weights, value_block, preferred_element_typ...  6.94 us
    all_to_all x1, starting transfers between devices, on_device(): lax.all_to_all(queries.reshape(tok_local, n_head, local_heads * DH), 'hea...  6.35 us
    all_to_all x1, waiting for transfers between devices, on_device(): lax.all_to_all(result, 'head', split_axis=0, concat_axis=2, tiled=True)  6.2 us
  transfers between devices with their start and end apart: 4, of which 3 were waited for; matrix products, arithmetic and copies ran while one was open for 8% of the time, Pallas kernels for 0%

commit v1 on v0

v1 whole, which is shorter than its diff:
```python
import functools
import math

import jax
import jax.numpy as jnp
from jax import lax
from jax.experimental import pallas as pl
from jax.experimental.pallas import tpu as pltpu
from jax.sharding import PartitionSpec as P

DH = 128
PAGE = 128
LANES = 128
TILE = 256
ROWS = DH + 8
BLOCK = 4
SCALE = 1.0 / math.sqrt(DH)
LOG2_SCALE = SCALE * math.log2(math.e)

lowest = -1e30
highest = 3e38


def attend(query, key_of, value_of, caps, pages, acc):
    acc[...] = jnp.zeros_like(acc)
    ones = jnp.ones((16, PAGE), jnp.bfloat16)

    def visit(block, best):
        maxima, outs = [], []
        for step in range(BLOCK):
            page = block * BLOCK + step
            scores = lax.dot_general(
                key_of(page), query, (((1,), (1,)), ((), ())), preferred_element_type=jnp.float32
            )
            page_max = jnp.max(scores, axis=0, keepdims=True)
            weights = jnp.exp2((scores - page_max) * LOG2_SCALE).astype(jnp.bfloat16)
            left = jnp.concatenate([value_of(page).T, ones], axis=0)
            outs.append(jnp.dot(left, weights, preferred_element_type=jnp.float32)[:ROWS])
            maxima.append(jnp.minimum(page_max, caps[page]))
        running = functools.reduce(jnp.maximum, maxima, best)
        joined = acc[...] * jnp.exp2((best - running) * LOG2_SCALE)
        for used_max, out in zip(maxima, outs):
            joined += out * jnp.exp2((used_max - running) * LOG2_SCALE)
        acc[...] = joined
        return running

    start = jnp.full((1, TILE), lowest, jnp.float32)
    return lax.fori_loop(0, pages // BLOCK, visit, start)


def kernel(plan, q_ref, k_hbm, v_hbm, caps, out_ref, k_buf, v_buf, acc, k_sem, v_sem):
    groups, heads_in, tiles_in, tile_blocks, n_cache = plan
    width = heads_in * DH
    pages = k_hbm.shape[0]
    head_blocks = groups // tile_blocks

    def load(block):
        columns = pl.ds(block * width, width)
        return (
            pltpu.make_async_copy(k_hbm.at[:, :, columns], k_buf.at[block], k_sem.at[block]),
            pltpu.make_async_copy(v_hbm.at[:, :, columns], v_buf.at[block], v_sem.at[block]),
        )

    for block in range(head_blocks):
        for copy in load(block):
            copy.start()
    for block in range(head_blocks):
        for copy in load(block):
            copy.wait()
        for tile_block in range(tile_blocks):
            group = block * tile_blocks + tile_block
            bests = []
            for unit in range(heads_in * tiles_in):
                head = unit // tiles_in
                columns = slice(head * DH, (head + 1) * DH)
                best = attend(
                    q_ref[group * heads_in * tiles_in + unit],
                    lambda page: k_buf[block, page, :, columns],
                    lambda page: v_buf[block, page, :, columns],
                    caps, pages, acc.at[unit],
                )
                bests.append(best)
            chunk = TILE // n_cache
            row = lax.broadcasted_iota(jnp.int32, (ROWS, TILE), 0)
            whole = [
                jnp.where(row == DH + 1, best, acc[unit]) for unit, best in enumerate(bests)
            ]
            for member in range(n_cache):
                piece = slice(member * chunk, (member + 1) * chunk)
                out_ref[group, member] = jnp.concatenate([part[:, piece] for part in whole], axis=1)


def on_device(queries, keys, values, page_lists, page_counts):
    n_head = lax.axis_size("head")
    n_cache = lax.axis_size("cache")
    tok_local = queries.shape[0]
    heads = keys.shape[2] // DH
    pages = keys.shape[0]
    share = tok_local // n_cache
    sources = TILE // tok_local
    tiles = n_head // sources
    units = LANES * n_cache // TILE
    tiles_in = min(units, tiles)
    heads_in = units // tiles_in
    tile_blocks = tiles // tiles_in
    head_blocks = heads // heads_in
    groups = head_blocks * tile_blocks
    moved = lax.all_to_all(
        queries.reshape(tok_local, n_head, heads * DH), "head", split_axis=1, concat_axis=0, tiled=True
    )
    moved = moved.reshape(tile_blocks, tiles_in, sources, n_cache, share, head_blocks, heads_in, DH)
    moved = moved.transpose(5, 0, 6, 1, 3, 2, 4, 7).reshape(groups * units, TILE, DH)
    used = jnp.arange(page_lists.shape[1], dtype=jnp.int32) < page_counts[0]
    ids = jnp.arange(pages, dtype=jnp.int32)
    live = jnp.any((page_lists[0][None, :] == ids[:, None]) & used[None, :], axis=1)
    caps = jnp.where(live, highest, lowest).astype(jnp.float32)
    plan = (groups, heads_in, tiles_in, tile_blocks, n_cache)
    width = heads_in * DH
    parts = pl.pallas_call(
        functools.partial(kernel, plan),
        out_shape=jax.ShapeDtypeStruct((groups, n_cache, ROWS, LANES), jnp.float32),
        in_specs=[
            pl.BlockSpec(memory_space=pltpu.VMEM),
            pl.BlockSpec(memory_space=pl.ANY),
            pl.BlockSpec(memory_space=pl.ANY),
            pl.BlockSpec(memory_space=pltpu.SMEM),
        ],
        out_specs=pl.BlockSpec(memory_space=pltpu.VMEM),
        scratch_shapes=[
            pltpu.VMEM((head_blocks, pages, PAGE, width), jnp.bfloat16),
            pltpu.VMEM((head_blocks, pages, PAGE, width), jnp.bfloat16),
            pltpu.VMEM((units, ROWS, TILE), jnp.float32),
            pltpu.SemaphoreType.DMA((head_blocks,)),
            pltpu.SemaphoreType.DMA((head_blocks,)),
        ],
        compiler_params=pltpu.CompilerParams(vmem_limit_bytes=56 * 1024 * 1024),
    )(moved, keys, values, caps)
    parts = lax.all_to_all(parts, "cache", split_axis=1, concat_axis=1, tiled=True)
    accum, total, best = parts[:, :, :DH], parts[:, :, DH], parts[:, :, DH + 1]
    top = jnp.max(best, axis=1, keepdims=True)
    keep = jnp.exp2((best - top) * LOG2_SCALE)
    total = jnp.sum(total * keep, axis=1)
    result = jnp.sum(accum * keep[:, :, None], axis=1) / total[:, None]
    logged = top[:, 0] * SCALE + jnp.log(total)
    lanes = (heads_in, tiles_in, sources, share)
    result = result.reshape(head_blocks, tile_blocks, DH, *lanes).transpose(1, 4, 5, 6, 0, 3, 2)
    logged = logged.reshape(head_blocks, tile_blocks, *lanes).transpose(1, 3, 4, 5, 0, 2)
    result = result.reshape(n_head, share, heads * DH)
    logged = logged.reshape(n_head, share, heads)
    result = lax.all_to_all(result, "head", split_axis=0, concat_axis=2, tiled=True)
    logged = lax.all_to_all(logged, "head", split_axis=0, concat_axis=2, tiled=True)
    return (result.reshape(share, -1), logged.reshape(share, -1))


def solution(mesh):
    in_specs = (
        P(("group", "head"), None),
        P(("group", "cache"), None, "head"),
        P(("group", "cache"), None, "head"),
        P(("group", "cache"), None),
        P(("group", "cache")),
    )
    out_specs = (P(("group", "head", "cache"), None), P(("group", "head", "cache"), None))
    return jax.shard_map(
        on_device, mesh=mesh, in_specs=in_specs, out_specs=out_specs, check_vma=False
    )
```

time: 246 us -> 114 us (0.46)
  blocking collectives: 110 us -> 17.7 us
  Pallas kernels: 0 us -> 47.1 us
  local copies, waits for them, and re-layouts: 49.7 us -> 8.9 us
  between operations: 14.8 us -> 1.4 us
  waiting for transfers between devices: 36.3 us -> 23.5 us
  other arithmetic: 11.2 us -> 1.58 us
  matrix products: 8.4 us -> 0 us
    all_gather x2 -> x0, blocking collectives: 110 us -> none  [combined_all(): pieces = jax.tree.map(lambda part: lax.all_gather(part, axis), value)]
    pallas_call x0 -> x1, Pallas kernels: none -> 47.1 us  [on_device(): pl.pallas_call(functools.partial(kernel, plan), out_shape=jax.ShapeDtypeS...]
    all_gather x1 -> x0, waiting for transfers between devices: 25.6 us -> none  [combined_all(): pieces = jax.tree.map(lambda part: lax.all_gather(part, axis), value)]
    all_to_all x0 -> x1, blocking collectives: none -> 17.7 us  [on_device(): lax.all_to_all(parts, 'cache', split_axis=1, concat_axis=1, tiled=True)]
    unnamed x8 -> x6, local copies, waits for them, and re-layouts: 19.1 us -> 2.28 us
    gather x4 -> x0, local copies, waits for them, and re-layouts: 16.5 us -> none  [the longest x2 8.26 us: visit_block(): value_block = pool_values[page_ids]]
    all_to_all x1, waiting for transfers between devices: 0.01 us -> 13.2 us  [on_device(): lax.all_to_all(queries.reshape(tok_local, n_head, heads * DH), 'head', sp...]
    dot_general x4 -> x0, matrix products: 8.4 us -> none  [the longest x2 6.94 us: visit_block(): jnp.einsum('thpk,pkhd->thpd', weights, value_block, preferred_element_typ...]
  transfers between devices with their start and end apart: 4 -> 3, of which waited for: 3 -> 3; matrix products, arithmetic and copies ran while one was open for 8% -> 3% of each run, Pallas kernels for 0% -> 0%
where the time goes in v1:
time: 114 us; the launch traced here: 113 us
  Pallas kernels  47.1 us (41%)
  waiting for transfers between devices  23.5 us (21%)
  blocking collectives  17.7 us (16%)
  starting transfers between devices  13 us (11%)
  local copies, waits for them, and re-layouts  8.9 us (8%)
  other arithmetic  1.58 us (1%)
  between operations  1.4 us (1%)
    pallas_call x1, Pallas kernels, on_device(): pl.pallas_call(functools.partial(kernel, plan), out_shape=jax.ShapeDtypeS...  47.1 us
    all_to_all x1, blocking collectives, on_device(): lax.all_to_all(parts, 'cache', split_axis=1, concat_axis=1, tiled=True)  17.7 us
    all_to_all x1, waiting for transfers between devices, on_device(): lax.all_to_all(queries.reshape(tok_local, n_head, heads * DH), 'head', sp...  13.2 us
    all_to_all x1, starting transfers between devices, on_device(): lax.all_to_all(queries.reshape(tok_local, n_head, heads * DH), 'head', sp...  6.35 us
    all_to_all x1, waiting for transfers between devices, on_device(): lax.all_to_all(result, 'head', split_axis=0, concat_axis=2, tiled=True)  6.15 us
    all_to_all x1, waiting for transfers between devices, on_device(): lax.all_to_all(logged, 'head', split_axis=0, concat_axis=2, tiled=True)  4.19 us
    all_to_all x1, starting transfers between devices, on_device(): lax.all_to_all(result, 'head', split_axis=0, concat_axis=2, tiled=True)  3.41 us
    all_to_all x1, starting transfers between devices, on_device(): lax.all_to_all(logged, 'head', split_axis=0, concat_axis=2, tiled=True)  3.22 us
  transfers between devices with their start and end apart: 3, of which 3 were waited for; matrix products, arithmetic and copies ran while one was open for 3% of the time, Pallas kernels for 0%

profile of v1, /device:TPU:0, one launch (start us, length us, event | category | flops | bytes accessed | tf_op | source)
XLA Modules:
  0.0 113.2 jit_solution(10392233498371870159)
XLA Ops:
  0.6 1.9 %copy.52 = bf16[8,4,8,1024]{3,2,0,1:T(8,128)(2,1)} copy(bf16[8,4,8,1024]{3,2,1,0:T(8,128)(2,1)} %bitcast.48) | data formatting | bytes 1048576 | tf_op jit(solution)/shard_map/reshape | solution.py:109
  2.5 6.3 %all-to-all-start = ((bf16[64,4,1024]{2,0,1:T(8,128)(2,1)}), bf16[64,4,1024]{2,0,1:T(8,128)(2,1)S(1)}, u32[]{:S(2)}, u32[]{:S(2)}) async-start(bf16[64,4,1024]{2,0,1:T(8,128)(2,1)} %bitcast.40), calls=%async_computation | async-start | bytes 1048576 | tf_op jit(solution)/shard_map/all_to_all | solution.py:108
  9.5 0.1 fusion.2
  9.7 0.5 broadcast_select_fusion.caps
  10.2 13.2 %all-to-all-done = bf16[64,4,1024]{2,0,1:T(8,128)(2,1)S(1)} async-done(((bf16[64,4,1024]{2,0,1:T(8,128)(2,1)}), bf16[64,4,1024]{2,0,1:T(8,128)(2,1)S(1)}, u32[]{:S(2)}, u32[]{:S(2)}) %all-to-all-start) | async-done | bytes 524320 | tf_op jit(solution)/shard_map/all_to_all | solution.py:108
  23.4 0.4 reshape.78
  23.7 0.9 copy.38
  24.6 47.1 %shard_map.68 = f32[4,4,136,128]{3,2,1,0:T(8,128)} custom-call(bf16[8,256,128]{2,1,0:T(8,128)(2,1)} %bitcast.42, bf16[32,128,1024]{2,1,0:T(8,128)(2,1)} %k_hbm.1, bf16[32,128,1024]{2,1,0:T(8,128)(2,1)} %v_hbm.1, f32[32]{0:T(128)} %broadcast_select_fusion.caps), custom_call_target="tpu_custom_call" | custom-call | tf_op jit(solution)/shard_map/pallas_call | solution.py:119
  71.8 1.3 %copy.39 = f32[4,4,136,128]{3,2,0,1:T(8,128)S(1)} copy(f32[4,4,136,128]{3,2,1,0:T(8,128)} %shard_map.68) | data formatting | bytes 2228224 | tf_op jit(solution)/shard_map/pallas_call | solution.py:119
  73.1 17.7 %all_to_all.50 = f32[4,4,136,128]{3,2,0,1:T(8,128)S(1)} all-to-all(f32[4,4,136,128]{3,2,0,1:T(8,128)S(1)} %copy.39), channel_id=1, replica_groups=mesh['group'=2,'head'=4,'cache'=4] {'cache'}, dimensions={1} | all-to-all | bytes 2228224 | tf_op jit(solution)/shard_map/all_to_all | solution.py:138
  91.1 0.1 copy.42
  91.3 0.7 reshape.84
  92.0 3.2 %all-to-all-start.3 = ((f32[4,1,128]{2,1,0:T(1,128)}), f32[4,1,128]{2,1,0:T(1,128)S(1)}, u32[]{:S(2)}, u32[]{:S(2)}) async-start(f32[4,1,128]{2,1,0:T(1,128)} %reshape.84), calls=%async_computation.3 | async-start | bytes 4096 | tf_op jit(solution)/shard_map/all_to_all | solution.py:151
  95.2 0.1 divide_bitcast_fusion
  95.3 0.2 copy.43
  95.5 0.9 reshape.80
  96.5 4.2 %all-to-all-done.3 = f32[4,1,128]{2,1,0:T(1,128)S(1)} async-done(((f32[4,1,128]{2,1,0:T(1,128)}), f32[4,1,128]{2,1,0:T(1,128)S(1)}, u32[]{:S(2)}, u32[]{:S(2)}) %all-to-all-start.3) | async-done | bytes 2080 | tf_op jit(solution)/shard_map/all_to_all | solution.py:151
  100.7 3.4 %all-to-all-start.2 = ((f32[4,16,1024]{2,1,0:T(8,128)}), f32[4,16,1024]{2,1,0:T(8,128)S(1)}, u32[]{:S(2)}, u32[]{:S(2)}) async-start(f32[4,16,1024]{2,1,0:T(8,128)} %reshape.80), calls=%async_computation.2 | async-start | bytes 524288 | tf_op jit(solution)/shard_map/all_to_all | solution.py:150
  104.1 0.5 broadcast.25
  104.6 0.7 reduce.1
  105.3 0.7 copy.46
  106.0 6.2 %all-to-all-done.2 = f32[4,16,1024]{2,1,0:T(8,128)S(1)} async-done(((f32[4,16,1024]{2,1,0:T(8,128)}), f32[4,16,1024]{2,1,0:T(8,128)S(1)}, u32[]{:S(2)}, u32[]{:S(2)}) %all-to-all-start.2) | async-done | bytes 262176 | tf_op jit(solution)/shard_map/all_to_all | solution.py:150
  112.2 0.2 copy.44
  112.3 0.9 copy.50
  (14 shorter events, 0.4 us)
Async XLA Ops:
  0.6 8.9 %copy-start = (s32[1,32]{1,0:T(1,128)S(1)}, s32[1,32]{1,0:T(1,128)}, u32[]{:S(2)}) copy-start(s32[1,32]{1,0:T(1,128)} %param.8) | copy-start | bytes 388
  2.5 20.8 %all-to-all-start = ((bf16[64,4,1024]{2,0,1:T(8,128)(2,1)}), bf16[64,4,1024]{2,0,1:T(8,128)(2,1)S(1)}, u32[]{:S(2)}, u32[]{:S(2)}) async-start(bf16[64,4,1024]{2,0,1:T(8,128)(2,1)} %bitcast.40), calls=%async_computation | async-start | bytes 1048576 | tf_op jit(solution)/shard_map/all_to_all | solution.py:108
  92.0 8.7 %all-to-all-start.3 = ((f32[4,1,128]{2,1,0:T(1,128)}), f32[4,1,128]{2,1,0:T(1,128)S(1)}, u32[]{:S(2)}, u32[]{:S(2)}) async-start(f32[4,1,128]{2,1,0:T(1,128)} %reshape.84), calls=%async_computation.3 | async-start | bytes 4096 | tf_op jit(solution)/shard_map/all_to_all | solution.py:151
  100.7 11.5 %all-to-all-start.2 = ((f32[4,16,1024]{2,1,0:T(8,128)}), f32[4,16,1024]{2,1,0:T(8,128)S(1)}, u32[]{:S(2)}, u32[]{:S(2)}) async-start(f32[4,16,1024]{2,1,0:T(8,128)} %reshape.80), calls=%async_computation.2 | async-start | bytes 524288 | tf_op jit(solution)/shard_map/all_to_all | solution.py:150

commit v2 on v1

v2 whole, which is shorter than its diff:
```python
import functools
import math

import jax
import jax.numpy as jnp
from jax import lax
from jax.experimental import pallas as pl
from jax.experimental.pallas import tpu as pltpu
from jax.sharding import PartitionSpec as P

DH = 128
PAGE = 128
LANES = 128
TILE = 256
ROWS = DH + 8
BLOCK = 4
SCALE = 1.0 / math.sqrt(DH)
LOG2_SCALE = SCALE * math.log2(math.e)

lowest = -1e30
highest = 3e38


def attend(queries, key_of, value_of, caps, pages, acc, scores):
    units = len(queries)
    acc[...] = jnp.zeros_like(acc)
    ones = jnp.ones((16, PAGE), jnp.bfloat16)
    blocks = pages // BLOCK

    def score(unit, page):
        return lax.dot_general(
            key_of(unit, page), queries[unit][...], (((1,), (1,)), ((), ())),
            preferred_element_type=jnp.float32,
        )

    for unit in range(units):
        for step in range(BLOCK):
            scores[unit, step] = score(unit, step)

    def visit(block, bests):
        after = jnp.minimum(block + 1, blocks - 1) * BLOCK
        runnings = []
        for unit in range(units):
            maxima, outs = [], []
            for step in range(BLOCK):
                page = block * BLOCK + step
                page_max = jnp.max(scores[unit, step], axis=0, keepdims=True)
                weights = jnp.exp2((scores[unit, step] - page_max) * LOG2_SCALE).astype(jnp.bfloat16)
                scores[unit, step] = score(unit, after + step)
                left = jnp.concatenate([value_of(unit, page).T, ones], axis=0)
                outs.append(jnp.dot(left, weights, preferred_element_type=jnp.float32)[:ROWS])
                maxima.append(jnp.minimum(page_max, caps[page]))
            running = functools.reduce(jnp.maximum, maxima, bests[unit])
            joined = acc[unit] * jnp.exp2((bests[unit] - running) * LOG2_SCALE)
            for used_max, out in zip(maxima, outs):
                joined += out * jnp.exp2((used_max - running) * LOG2_SCALE)
            acc[unit] = joined
            runnings.append(running)
        return tuple(runnings)

    start = jnp.full((1, TILE), lowest, jnp.float32)
    return lax.fori_loop(0, blocks, visit, (start,) * units)


def kernel(
    plan, q_ref, k_hbm, v_hbm, caps, out_ref, log_ref,
    k_buf, v_buf, q_all, q_units, acc, scores, part_out, part_in, piece_out, piece_in, log_out, log_in,
    k_sem, v_sem, own_sem, q_send, q_recv, part_send, part_recv, piece_send, piece_recv, log_send, log_recv,
):
    groups, heads_in, tiles_in, tile_blocks, n_head, n_cache, heads, sources = plan
    units = heads_in * tiles_in
    width = heads_in * DH
    pages = k_hbm.shape[0]
    head_blocks = groups // tile_blocks
    share = q_ref.shape[0] // n_cache
    chunk = TILE // n_cache
    spread = tiles_in * sources
    me = lax.axis_index("head")
    seat = lax.axis_index("cache")

    def load(block):
        columns = pl.ds(pl.multiple_of(block * width, DH), width)
        return (
            pltpu.make_async_copy(k_hbm.at[:, :, columns], k_buf.at[block], k_sem.at[block]),
            pltpu.make_async_copy(v_hbm.at[:, :, columns], v_buf.at[block], v_sem.at[block]),
        )

    def peer_of(index, count, offset):
        return lax.rem(index + offset, count)

    def query_source(block, owner):
        return q_ref.at[:, pl.ds(pl.multiple_of(owner * heads * DH + block * width, DH), width)]

    def own_query(block):
        return pltpu.make_async_copy(query_source(block, me), q_all.at[block, me], own_sem.at[block])

    def query_copy(block, offset, source):
        peer = peer_of(me, n_head, offset)
        return pltpu.make_async_remote_copy(
            src_ref=query_source(block, peer), dst_ref=q_all.at[block, source],
            send_sem=q_send.at[block, offset - 1], recv_sem=q_recv.at[block, source],
            device_id={"head": peer}, device_id_type=pl.DeviceIdType.MESH,
        )

    def part_copy(group, offset, source):
        peer = peer_of(seat, n_cache, offset)
        return pltpu.make_async_remote_copy(
            src_ref=part_out.at[group, peer], dst_ref=part_in.at[group, source],
            send_sem=part_send.at[group, offset - 1], recv_sem=part_recv.at[group, source],
            device_id={"cache": peer}, device_id_type=pl.DeviceIdType.MESH,
        )

    def piece_copy(group, place, source):
        target = group % tile_blocks * spread + place
        block = group // tile_blocks
        return target, pltpu.make_async_remote_copy(
            src_ref=piece_out.at[group, place], dst_ref=piece_in.at[block, source],
            send_sem=piece_send.at[group, place], recv_sem=piece_recv.at[block, source],
            device_id={"head": target}, device_id_type=pl.DeviceIdType.MESH,
        )

    def log_copy(offset, source):
        peer = peer_of(me, n_head, offset)
        return pltpu.make_async_remote_copy(
            src_ref=log_out.at[peer], dst_ref=log_in.at[source],
            send_sem=log_send.at[offset - 1], recv_sem=log_recv.at[source],
            device_id={"head": peer}, device_id_type=pl.DeviceIdType.MESH,
        )

    for copy in load(0):
        copy.start()
    barrier = pltpu.get_barrier_semaphore()
    for offset in range(1, n_head):
        pl.semaphore_signal(
            barrier, inc=1, device_id={"head": peer_of(me, n_head, offset)},
            device_id_type=pl.DeviceIdType.MESH,
        )
    for offset in range(1, n_cache):
        pl.semaphore_signal(
            barrier, inc=1, device_id={"cache": peer_of(seat, n_cache, offset)},
            device_id_type=pl.DeviceIdType.MESH,
        )
    for block in range(head_blocks):
        own_query(block).start()
        if block:
            for copy in load(block):
                copy.start()
    pl.semaphore_wait(barrier, n_head + n_cache - 2)
    for block in range(head_blocks):
        for offset in range(1, n_head):
            query_copy(block, offset, me).start()
    log_out[...] = jnp.zeros_like(log_out)

    def ready(block):
        for copy in load(block):
            copy.wait()
        own_query(block).wait()
        for offset in range(1, n_head):
            query_copy(block, offset, peer_of(me, n_head, offset)).wait_recv()

    def compute(group):
        block = group // tile_blocks
        if tile_blocks == 1:
            ready(block)
        else:
            pl.when(group % tile_blocks == 0)(lambda: ready(block))

        def column(unit):
            return slice(unit // tiles_in * DH, (unit // tiles_in + 1) * DH)

        for unit in range(units):
            first = (group % tile_blocks * tiles_in + unit % tiles_in) * sources
            rows = [q_all[block, first + l, :, column(unit)].astype(jnp.float32) for l in range(sources)]
            ordered = [
                row[c * share:(c + 1) * share] for c in range(n_cache) for row in rows
            ]
            q_units[unit] = jnp.concatenate(ordered, axis=0).astype(jnp.bfloat16)
        bests = attend(
            [q_units.at[unit] for unit in range(units)],
            lambda unit, page: k_buf[block, page, :, column(unit)],
            lambda unit, page: v_buf[block, page, :, column(unit)],
            caps, pages, acc, scores,
        )
        row = lax.broadcasted_iota(jnp.int32, (8, TILE), 0)
        tails = [jnp.where(row == 1, best, acc[unit, DH:ROWS]) for unit, best in enumerate(bests)]
        for member in range(n_cache):
            piece = slice(member * chunk, (member + 1) * chunk)
            part_out[group, member, :DH] = jnp.concatenate(
                [acc[unit, :DH, piece] for unit in range(units)], axis=1
            )
            part_out[group, member, DH:ROWS] = jnp.concatenate([tail[:, piece] for tail in tails], axis=1)
        for offset in range(1, n_cache):
            part_copy(group, offset, seat).start()
        part_in[group, seat] = part_out[group, seat]

    def finish(group):
        block = group // tile_blocks
        for offset in range(1, n_cache):
            part_copy(group, offset, peer_of(seat, n_cache, offset)).wait_recv()
        totals = [part_in[group, c, DH:DH + 1] for c in range(n_cache)]
        bests = [part_in[group, c, DH + 1:DH + 2] for c in range(n_cache)]
        top = functools.reduce(jnp.maximum, bests)
        keeps = [jnp.exp2((best - top) * LOG2_SCALE) for best in bests]
        total = functools.reduce(jnp.add, [t * keep for t, keep in zip(totals, keeps)])
        inverse = 1.0 / total
        result = functools.reduce(
            jnp.add, [part_in[group, c, :DH] * (keep * inverse) for c, keep in enumerate(keeps)]
        ).T
        logged = jnp.broadcast_to(top * SCALE + jnp.log(total), (LANES, LANES)).T
        lane = lax.broadcasted_iota(jnp.int32, (share, LANES), 1)
        for unit in range(units):
            head = unit // tiles_in
            for l in range(sources):
                place = unit % tiles_in * sources + l
                at = unit * sources * share + l * share
                piece_out[group, place, :, head * DH:(head + 1) * DH] = result[at:at + share]
                target = group % tile_blocks * spread + place
                log_out[target] += jnp.where(
                    lane == me * heads + block * heads_in + head, logged[at:at + share], 0.0
                )
        for place in range(spread):
            target, copy = piece_copy(group, place, me)
            pl.when(target != me)(copy.start)

            @pl.when(target == me)
            def _():
                piece_in[block, me] = piece_out[group, place]

    compute(0)

    def step(group, carry):
        compute(group)
        finish(group - 1)
        return carry

    lax.fori_loop(1, groups, step, 0)
    finish(groups - 1)
    for offset in range(1, n_head):
        log_copy(offset, me).start()
    log_in[me] = log_out[me]
    for block in range(head_blocks):
        for offset in range(1, n_head):
            query_copy(block, offset, me).wait_send()
    for group in range(groups):
        for offset in range(1, n_cache):
            part_copy(group, offset, seat).wait_send()
    for block in range(head_blocks):
        for offset in range(1, n_head):
            source = peer_of(me, n_head, offset)
            pltpu.make_async_remote_copy(
                src_ref=piece_out.at[block, 0], dst_ref=piece_in.at[block, source],
                send_sem=piece_send.at[block, 0], recv_sem=piece_recv.at[block, source],
                device_id={"head": source}, device_id_type=pl.DeviceIdType.MESH,
            ).wait_recv()
        for source in range(n_head):
            at = (source * heads + block * heads_in) * DH
            out_ref[:, at:at + width] = piece_in[block, source]
    for offset in range(1, n_head):
        log_copy(offset, peer_of(me, n_head, offset)).wait_recv()
    log_ref[...] = functools.reduce(jnp.add, [log_in[s] for s in range(n_head)])[:, :log_ref.shape[1]]
    for group in range(groups):
        for place in range(spread):
            target, copy = piece_copy(group, place, me)
            pl.when(target != me)(copy.wait_send)
    for offset in range(1, n_head):
        log_copy(offset, me).wait_send()


def on_device(queries, keys, values, page_lists, page_counts):
    n_head = lax.axis_size("head")
    n_cache = lax.axis_size("cache")
    tok_local = queries.shape[0]
    heads = keys.shape[2] // DH
    pages = keys.shape[0]
    share = tok_local // n_cache
    sources = TILE // tok_local
    tiles = n_head // sources
    units = LANES * n_cache // TILE
    tiles_in = min(units, tiles)
    heads_in = units // tiles_in
    tile_blocks = tiles // tiles_in
    head_blocks = heads // heads_in
    groups = head_blocks * tile_blocks
    spread = tiles_in * sources
    width = heads_in * DH
    used = jnp.arange(page_lists.shape[1], dtype=jnp.int32) < page_counts[0]
    ids = jnp.arange(pages, dtype=jnp.int32)
    live = jnp.any((page_lists[0][None, :] == ids[:, None]) & used[None, :], axis=1)
    caps = jnp.where(live, highest, lowest).astype(jnp.float32)
    plan = (groups, heads_in, tiles_in, tile_blocks, n_head, n_cache, heads, sources)
    dma = pltpu.SemaphoreType.DMA
    return pl.pallas_call(
        functools.partial(kernel, plan),
        out_shape=(
            jax.ShapeDtypeStruct((share, queries.shape[1]), jnp.float32),
            jax.ShapeDtypeStruct((share, n_head * heads), jnp.float32),
        ),
        in_specs=[
            pl.BlockSpec(memory_space=pltpu.VMEM),
            pl.BlockSpec(memory_space=pl.ANY),
            pl.BlockSpec(memory_space=pl.ANY),
            pl.BlockSpec(memory_space=pltpu.SMEM),
        ],
        out_specs=(pl.BlockSpec(memory_space=pltpu.VMEM), pl.BlockSpec(memory_space=pltpu.VMEM)),
        scratch_shapes=[
            pltpu.VMEM((head_blocks, pages, PAGE, width), jnp.bfloat16),
            pltpu.VMEM((head_blocks, pages, PAGE, width), jnp.bfloat16),
            pltpu.VMEM((head_blocks, n_head, tok_local, width), jnp.bfloat16),
            pltpu.VMEM((units, TILE, DH), jnp.bfloat16),
            pltpu.VMEM((units, ROWS, TILE), jnp.float32),
            pltpu.VMEM((units, BLOCK, PAGE, TILE), jnp.float32),
            pltpu.VMEM((groups, n_cache, ROWS, LANES), jnp.float32),
            pltpu.VMEM((groups, n_cache, ROWS, LANES), jnp.float32),
            pltpu.VMEM((groups, spread, share, width), jnp.float32),
            pltpu.VMEM((head_blocks, n_head, share, width), jnp.float32),
            pltpu.VMEM((n_head, share, LANES), jnp.float32),
            pltpu.VMEM((n_head, share, LANES), jnp.float32),
            dma((head_blocks,)),
            dma((head_blocks,)),
            dma((head_blocks,)),
            dma((head_blocks, n_head - 1)),
            dma((head_blocks, n_head)),
            dma((groups, n_cache - 1)),
            dma((groups, n_cache)),
            dma((groups, spread)),
            dma((head_blocks, n_head)),
            dma((n_head - 1,)),
            dma((n_head,)),
        ],
        compiler_params=pltpu.CompilerParams(
            collective_id=0, has_side_effects=True, vmem_limit_bytes=56 * 1024 * 1024
        ),
    )(queries, keys, values, caps)


def solution(mesh):
    in_specs = (
        P(("group", "head"), None),
        P(("group", "cache"), None, "head"),
        P(("group", "cache"), None, "head"),
        P(("group", "cache"), None),
        P(("group", "cache")),
    )
    out_specs = (P(("group", "head", "cache"), None), P(("group", "head", "cache"), None))
    return jax.shard_map(
        on_device, mesh=mesh, in_specs=in_specs, out_specs=out_specs, check_vma=False
    )
```

time: 114 us -> 46.5 us (0.41)
  waiting for transfers between devices: 23.5 us -> 0 us
  blocking collectives: 17.7 us -> 0 us
  starting transfers between devices: 13 us -> 0 us
  Pallas kernels: 47.1 us -> 40.7 us
  local copies, waits for them, and re-layouts: 8.9 us -> 2.97 us
    all_to_all x3 -> x0, waiting for transfers between devices: 23.5 us -> none  [the longest x1 13.2 us: on_device(): lax.all_to_all(queries.reshape(tok_local, n_head, heads * DH), 'head', sp...]
    all_to_all x1 -> x0, blocking collectives: 17.7 us -> none  [on_device(): lax.all_to_all(parts, 'cache', split_axis=1, concat_axis=1, tiled=True)]
    all_to_all x3 -> x0, starting transfers between devices: 13 us -> none  [the longest x1 6.35 us: on_device(): lax.all_to_all(queries.reshape(tok_local, n_head, heads * DH), 'head', sp...]
    pallas_call x1, Pallas kernels: 47.1 us -> 40.7 us  [on_device(): pl.pallas_call(functools.partial(kernel, plan), out_shape=(jax.ShapeDtype...]
    reshape x4 -> x0, local copies, waits for them, and re-layouts: 3.16 us -> none  [the longest x1 1.88 us: on_device(): queries.reshape(tok_local, n_head, heads * DH)]
    pallas_call x1 -> x0, local copies, waits for them, and re-layouts: 1.32 us -> none  [on_device(): pl.pallas_call(functools.partial(kernel, plan), out_shape=jax.ShapeDtypeS...]
    unnamed x6 -> x2, local copies, waits for them, and re-layouts: 2.28 us -> 2.97 us
  transfers between devices with their start and end apart: 3 -> 0, of which waited for: 3 -> 0; matrix products, arithmetic and copies ran while one was open for 3% -> 0% of each run, Pallas kernels for 0% -> 0%
where the time goes in v2:
time: 46.5 us; the launch traced here: 46.2 us
  Pallas kernels  40.7 us (88%)
  local copies, waits for them, and re-layouts  2.97 us (6%)
  other arithmetic  1.3 us (3%)
  between operations  1.29 us (3%)
    pallas_call x1, Pallas kernels, on_device(): pl.pallas_call(functools.partial(kernel, plan), out_shape=(jax.ShapeDtype...  40.7 us
    unnamed x2, local copies, waits for them, and re-layouts  2.97 us

profile of v2, /device:TPU:0, one launch (start us, length us, event | category | flops | bytes accessed | tf_op | source)
XLA Modules:
  0.0 46.2 jit_solution(12316056043658147121)
XLA Ops:
  1.3 0.8 %fusion.1 = pred[32]{0:T(512)(128)(4,1)S(1)} fusion(s32[32]{0:T(128)} %bitcast.3, pred[32]{0:T(512)(128)(4,1)S(1)} %iota_compare_fusion.1), kind=kLoop, calls=%fused_computation.2 | loop fusion | flops 3040 | bytes 192 | tf_op jit(solution)/shard_map/reduce_or | solution.py:288
  2.1 0.5 %broadcast_select_fusion.caps = f32[32]{0:T(128)} fusion(pred[32]{0:T(512)(128)(4,1)S(1)} %fusion.1), kind=kLoop, calls=%fused_computation.4 | loop fusion | flops 32 | bytes 160 | tf_op jit(solution)/shard_map/jit(_where)/select_n | solution.py:289
  2.6 40.7 %shard_map.68 = (f32[16,4096]{1,0:T(8,128)}, f32[16,32]{1,0:T(8,128)}) custom-call(bf16[64,4096]{1,0:T(8,128)(2,1)} %q_ref.1, bf16[32,128,1024]{2,1,0:T(8,128)(2,1)} %k_hbm.1, bf16[32,128,1024]{2,1,0:T(8,128)(2,1)} %v_hbm.1, f32[32]{0:T(128)} %broadcast_select_fusion.caps), custom_call_target="tpu_custom_call" | custom-call | tf_op jit(solution)/shard_map/pallas_call | solution.py:292
  43.3 1.7 %copy.10 = f32[16,4096]{1,0:T(8,128)} copy(f32[16,4096]{1,0:T(8,128)} %get-tuple-element.4) | data formatting | bytes 524288
  44.9 1.3 %copy.11 = f32[16,32]{1,0:T(8,128)} copy(f32[16,32]{1,0:T(8,128)} %get-tuple-element.5) | data formatting | bytes 4096
  (1 shorter events, 0.0 us)

commit v3 on v2

--- a/solution.py
+++ b/solution.py
@@ -13,7 +13,7 @@
 LANES = 128
 TILE = 256
 ROWS = DH + 8
-BLOCK = 4
+BLOCK = 8
 SCALE = 1.0 / math.sqrt(DH)
 LOG2_SCALE = SCALE * math.log2(math.e)
 
@@ -28,17 +28,16 @@
     blocks = pages // BLOCK
 
     def score(unit, page):
+        rows = key_of(unit, pl.ds(page, BLOCK)).reshape(BLOCK * PAGE, DH)
         return lax.dot_general(
-            key_of(unit, page), queries[unit][...], (((1,), (1,)), ((), ())),
+            rows, queries[unit][...], (((1,), (1,)), ((), ())),
             preferred_element_type=jnp.float32,
-        )
+        ).reshape(BLOCK, PAGE, TILE)
 
     for unit in range(units):
-        for step in range(BLOCK):
-            scores[unit, step] = score(unit, step)
-
-    def visit(block, bests):
-        after = jnp.minimum(block + 1, blocks - 1) * BLOCK
+        scores[unit] = score(unit, 0)
+
+    def visit(block, bests, more=True):
         runnings = []
         for unit in range(units):
             maxima, outs = [], []
@@ -46,10 +45,11 @@
                 page = block * BLOCK + step
                 page_max = jnp.max(scores[unit, step], axis=0, keepdims=True)
                 weights = jnp.exp2((scores[unit, step] - page_max) * LOG2_SCALE).astype(jnp.bfloat16)
-                scores[unit, step] = score(unit, after + step)
                 left = jnp.concatenate([value_of(unit, page).T, ones], axis=0)
                 outs.append(jnp.dot(left, weights, preferred_element_type=jnp.float32)[:ROWS])
-                maxima.append(jnp.minimum(page_max, caps[page]))
+                maxima.append(jnp.minimum(page_max, caps[pl.ds(page, 1), :]))
+            if more:
+                scores[unit] = score(unit, (block + 1) * BLOCK)
             running = functools.reduce(jnp.maximum, maxima, bests[unit])
             joined = acc[unit] * jnp.exp2((bests[unit] - running) * LOG2_SCALE)
             for used_max, out in zip(maxima, outs):
@@ -59,12 +59,13 @@
         return tuple(runnings)
 
     start = jnp.full((1, TILE), lowest, jnp.float32)
-    return lax.fori_loop(0, blocks, visit, (start,) * units)
+    bests = lax.fori_loop(0, blocks - 1, visit, (start,) * units)
+    return visit(blocks - 1, bests, more=False)
 
 
 def kernel(
-    plan, q_ref, k_hbm, v_hbm, caps, out_ref, log_ref,
-    k_buf, v_buf, q_all, q_units, acc, scores, part_out, part_in, piece_out, piece_in, log_out, log_in,
+    plan, q_ref, k_hbm, v_hbm, lists, counts, out_ref, log_ref,
+    caps, k_buf, v_buf, q_all, q_units, acc, scores, part_out, part_in, piece_out, piece_in, log_out, log_in,
     k_sem, v_sem, own_sem, q_send, q_recv, part_send, part_recv, piece_send, piece_recv, log_send, log_recv,
 ):
     groups, heads_in, tiles_in, tile_blocks, n_head, n_cache, heads, sources = plan
@@ -150,6 +151,12 @@
         for offset in range(1, n_head):
             query_copy(block, offset, me).start()
     log_out[...] = jnp.zeros_like(log_out)
+    slots = lists.shape[1]
+    used = lax.broadcasted_iota(jnp.int32, (1, slots), 1) < counts[0]
+    listed = jnp.where(used, lists[...], -1)
+    match = listed == lax.broadcasted_iota(jnp.int32, (pages, slots), 0)
+    cap = jnp.max(jnp.where(match, highest, lowest), axis=1, keepdims=True)
+    caps[...] = jnp.broadcast_to(cap, caps.shape)
 
     def ready(block):
         for copy in load(block):
@@ -226,14 +233,12 @@
             def _():
                 piece_in[block, me] = piece_out[group, place]
 
-    compute(0)
-
     def step(group, carry):
         compute(group)
-        finish(group - 1)
+        pl.when(group > 0)(lambda: finish(group - 1))
         return carry
 
-    lax.fori_loop(1, groups, step, 0)
+    lax.fori_loop(0, groups, step, 0)
     finish(groups - 1)
     for offset in range(1, n_head):
         log_copy(offset, me).start()
@@ -266,6 +271,17 @@
         log_copy(offset, me).wait_send()
 
 
+def settle(attended, logged, out_ref, log_ref, sem):
+    copies = (
+        pltpu.make_async_copy(attended, out_ref, sem.at[0]),
+        pltpu.make_async_copy(logged, log_ref, sem.at[1]),
+    )
+    for copy in copies:
+        copy.start()
+    for copy in copies:
+        copy.wait()
+
+
 def on_device(queries, keys, values, page_lists, page_counts):
     n_head = lax.axis_size("head")
     n_cache = lax.axis_size("cache")
@@ -283,13 +299,9 @@
     groups = head_blocks * tile_blocks
     spread = tiles_in * sources
     width = heads_in * DH
-    used = jnp.arange(page_lists.shape[1], dtype=jnp.int32) < page_counts[0]
-    ids = jnp.arange(pages, dtype=jnp.int32)
-    live = jnp.any((page_lists[0][None, :] == ids[:, None]) & used[None, :], axis=1)
-    caps = jnp.where(live, highest, lowest).astype(jnp.float32)
     plan = (groups, heads_in, tiles_in, tile_blocks, n_head, n_cache, heads, sources)
     dma = pltpu.SemaphoreType.DMA
-    return pl.pallas_call(
+    attended, logged = pl.pallas_call(
         functools.partial(kernel, plan),
         out_shape=(
             jax.ShapeDtypeStruct((share, queries.shape[1]), jnp.float32),
@@ -299,10 +311,12 @@
             pl.BlockSpec(memory_space=pltpu.VMEM),
             pl.BlockSpec(memory_space=pl.ANY),
             pl.BlockSpec(memory_space=pl.ANY),
+            pl.BlockSpec(memory_space=pltpu.VMEM),
             pl.BlockSpec(memory_space=pltpu.SMEM),
         ],
         out_specs=(pl.BlockSpec(memory_space=pltpu.VMEM), pl.BlockSpec(memory_space=pltpu.VMEM)),
         scratch_shapes=[
+            pltpu.VMEM((pages, TILE), jnp.float32),
             pltpu.VMEM((head_blocks, pages, PAGE, width), jnp.bfloat16),
             pltpu.VMEM((head_blocks, pages, PAGE, width), jnp.bfloat16),
             pltpu.VMEM((head_blocks, n_head, tok_local, width), jnp.bfloat16),
@@ -330,7 +344,18 @@
         compiler_params=pltpu.CompilerParams(
             collective_id=0, has_side_effects=True, vmem_limit_bytes=56 * 1024 * 1024
         ),
-    )(queries, keys, values, caps)
+    )(queries, keys, values, page_lists, page_counts)
+    any_place = pl.BlockSpec(memory_space=pl.ANY)
+    return pl.pallas_call(
+        settle,
+        out_shape=(
+            jax.ShapeDtypeStruct(attended.shape, jnp.float32),
+            jax.ShapeDtypeStruct(logged.shape, jnp.float32),
+        ),
+        in_specs=[pl.BlockSpec(memory_space=pltpu.VMEM)] * 2,
+        out_specs=(any_place, any_place),
+        scratch_shapes=[dma((2,))],
+    )(attended, logged)
 
 
 def solution(mesh):

time: 46.5 us -> 42.4 us (0.912)
  local copies, waits for them, and re-layouts: 2.97 us -> 0 us
  other arithmetic: 1.3 us -> 0 us
    unnamed x2 -> x0, local copies, waits for them, and re-layouts: 2.97 us -> none
    pallas_call x0 -> x1, Pallas kernels: none -> 1.67 us  [on_device(): pl.pallas_call(settle, out_shape=(jax.ShapeDtypeStruct(attended.shape, jn...]
    pallas_call x1, Pallas kernels: 40.7 us -> 39.3 us  [on_device(): pl.pallas_call(functools.partial(kernel, plan), out_shape=(jax.ShapeDtype...]
    reduce_or x1 -> x0, other arithmetic: 0.77 us -> none  [on_device(): jnp.any((page_lists[0][None, :] == ids[:, None]) & used[None, :], axis=1)]
    select_n x1 -> x0, other arithmetic: 0.52 us -> none  [on_device(): caps = jnp.where(live, highest, lowest).astype(jnp.float32)]
where the time goes in v3:
time: 42.4 us; the launch traced here: 42.2 us
  Pallas kernels  40.9 us (96%)
  between operations  1.29 us (3%)
    pallas_call x1, Pallas kernels, on_device(): pl.pallas_call(functools.partial(kernel, plan), out_shape=(jax.ShapeDtype...  39.3 us
    pallas_call x1, Pallas kernels, on_device(): pl.pallas_call(settle, out_shape=(jax.ShapeDtypeStruct(attended.shape, jn...  1.67 us

profile of v3, /device:TPU:0, one launch (start us, length us, event | category | flops | bytes accessed | tf_op | source)
XLA Modules:
  0.0 42.2 jit_solution(15358581403901680256)
XLA Ops:
  1.3 39.3 %shard_map.68 = (f32[16,4096]{1,0:T(8,128)}, f32[16,32]{1,0:T(8,128)}) custom-call(bf16[64,4096]{1,0:T(8,128)(2,1)} %q_ref.1, bf16[32,128,1024]{2,1,0:T(8,128)(2,1)} %k_hbm.1, bf16[32,128,1024]{2,1,0:T(8,128)(2,1)} %v_hbm.1, s32[1,32]{1,0:T(1,128)} %lists.1, s32[1]{0:T(128)S(6)} %copy.7.counts), custom_call_target="tpu_custom_call" | custom-call | tf_op jit(solution)/shard_map/pallas_call | solution.py:304
  40.5 1.7 %shard_map.69 = (f32[16,4096]{1,0:T(8,128)}, f32[16,32]{1,0:T(8,128)}) custom-call(f32[16,4096]{1,0:T(8,128)} %get-tuple-element.4.attended, f32[16,32]{1,0:T(8,128)} %get-tuple-element.5.logged), custom_call_target="tpu_custom_call" | custom-call | tf_op jit(solution)/shard_map/pallas_call | solution.py:349

commit v4 on v3

--- a/solution.py
+++ b/solution.py
@@ -143,13 +143,9 @@
         )
     for block in range(head_blocks):
         own_query(block).start()
-        if block:
-            for copy in load(block):
-                copy.start()
     pl.semaphore_wait(barrier, n_head + n_cache - 2)
-    for block in range(head_blocks):
-        for offset in range(1, n_head):
-            query_copy(block, offset, me).start()
+    for offset in range(1, n_head):
+        query_copy(0, offset, me).start()
     log_out[...] = jnp.zeros_like(log_out)
     slots = lists.shape[1]
     used = lax.broadcasted_iota(jnp.int32, (1, slots), 1) < counts[0]
@@ -164,6 +160,13 @@
         own_query(block).wait()
         for offset in range(1, n_head):
             query_copy(block, offset, peer_of(me, n_head, offset)).wait_recv()
+
+        @pl.when(block + 1 < head_blocks)
+        def _():
+            for copy in load(block + 1):
+                copy.start()
+            for offset in range(1, n_head):
+                query_copy(block + 1, offset, me).start()
 
     def compute(group):
         block = group // tile_blocks

time: 42.4 us -> 40.6 us (0.958)
  Pallas kernels: 40.9 us -> 39.1 us
    pallas_call x1, Pallas kernels: 39.3 us -> 37.4 us  [on_device(): pl.pallas_call(functools.partial(kernel, plan), out_shape=(jax.ShapeDtype...]
where the time goes in v4:
time: 40.6 us; the launch traced here: 40.4 us
  Pallas kernels  39.1 us (96%)
  between operations  1.29 us (3%)
    pallas_call x1, Pallas kernels, on_device(): pl.pallas_call(functools.partial(kernel, plan), out_shape=(jax.ShapeDtype...  37.4 us
    pallas_call x1, Pallas kernels, on_device(): pl.pallas_call(settle, out_shape=(jax.ShapeDtypeStruct(attended.shape, jn...  1.67 us

profile of v4, /device:TPU:0, one launch (start us, length us, event | category | flops | bytes accessed | tf_op | source)
XLA Modules:
  0.0 40.4 jit_solution(3981074633943275889)
XLA Ops:
  1.3 37.4 %shard_map.68 = (f32[16,4096]{1,0:T(8,128)}, f32[16,32]{1,0:T(8,128)}) custom-call(bf16[64,4096]{1,0:T(8,128)(2,1)} %q_ref.1, bf16[32,128,1024]{2,1,0:T(8,128)(2,1)} %k_hbm.1, bf16[32,128,1024]{2,1,0:T(8,128)(2,1)} %v_hbm.1, s32[1,32]{1,0:T(1,128)} %lists.1, s32[1]{0:T(128)S(6)} %copy.7.counts), custom_call_target="tpu_custom_call" | custom-call | tf_op jit(solution)/shard_map/pallas_call | solution.py:307
  38.7 1.7 %shard_map.69 = (f32[16,4096]{1,0:T(8,128)}, f32[16,32]{1,0:T(8,128)}) custom-call(f32[16,4096]{1,0:T(8,128)} %get-tuple-element.4.attended, f32[16,32]{1,0:T(8,128)} %get-tuple-element.5.logged), custom_call_target="tpu_custom_call" | custom-call | tf_op jit(solution)/shard_map/pallas_call | solution.py:352

commit v5 on v4

--- a/solution.py
+++ b/solution.py
@@ -274,17 +274,6 @@
         log_copy(offset, me).wait_send()
 
 
-def settle(attended, logged, out_ref, log_ref, sem):
-    copies = (
-        pltpu.make_async_copy(attended, out_ref, sem.at[0]),
-        pltpu.make_async_copy(logged, log_ref, sem.at[1]),
-    )
-    for copy in copies:
-        copy.start()
-    for copy in copies:
-        copy.wait()
-
-
 def on_device(queries, keys, values, page_lists, page_counts):
     n_head = lax.axis_size("head")
     n_cache = lax.axis_size("cache")
@@ -307,8 +296,8 @@
     attended, logged = pl.pallas_call(
         functools.partial(kernel, plan),
         out_shape=(
-            jax.ShapeDtypeStruct((share, queries.shape[1]), jnp.float32),
-            jax.ShapeDtypeStruct((share, n_head * heads), jnp.float32),
+            pltpu.VMEM((share, queries.shape[1]), jnp.float32),
+            pltpu.VMEM((share, n_head * heads), jnp.float32),
         ),
         in_specs=[
             pl.BlockSpec(memory_space=pltpu.VMEM),
@@ -348,17 +337,7 @@
             collective_id=0, has_side_effects=True, vmem_limit_bytes=56 * 1024 * 1024
         ),
     )(queries, keys, values, page_lists, page_counts)
-    any_place = pl.BlockSpec(memory_space=pl.ANY)
-    return pl.pallas_call(
-        settle,
-        out_shape=(
-            jax.ShapeDtypeStruct(attended.shape, jnp.float32),
-            jax.ShapeDtypeStruct(logged.shape, jnp.float32),
-        ),
-        in_specs=[pl.BlockSpec(memory_space=pltpu.VMEM)] * 2,
-        out_specs=(any_place, any_place),
-        scratch_shapes=[dma((2,))],
-    )(attended, logged)
+    return attended, logged
 
 
 def solution(mesh):

time: 40.6 us -> 39.5 us (0.973)
  Pallas kernels: 39.1 us -> 36.7 us
  local copies, waits for them, and re-layouts: 0 us -> 1.3 us
    pallas_call x2 -> x1, Pallas kernels: 39.1 us -> 36.7 us  [on_device(): pl.pallas_call(functools.partial(kernel, plan), out_shape=(pltpu.VMEM((sh...]
    unnamed x0 -> x2, local copies, waits for them, and re-layouts: none -> 1.3 us
where the time goes in v5:
time: 39.5 us; the launch traced here: 39.3 us
  Pallas kernels  36.7 us (93%)
  local copies, waits for them, and re-layouts  1.3 us (3%)
  between operations  1.29 us (3%)
    pallas_call x1, Pallas kernels, on_device(): pl.pallas_call(functools.partial(kernel, plan), out_shape=(pltpu.VMEM((sh...  36.7 us
    unnamed x2, local copies, waits for them, and re-layouts  1.3 us

profile of v5, /device:TPU:0, one launch (start us, length us, event | category | flops | bytes accessed | tf_op | source)
XLA Modules:
  0.0 39.3 jit_solution(4520985504636051178)
XLA Ops:
  1.3 36.7 %shard_map.68 = (f32[16,4096]{1,0:T(8,128)S(1)}, f32[16,32]{1,0:T(8,128)S(1)}) custom-call(bf16[64,4096]{1,0:T(8,128)(2,1)} %q_ref.1, bf16[32,128,1024]{2,1,0:T(8,128)(2,1)} %k_hbm.1, bf16[32,128,1024]{2,1,0:T(8,128)(2,1)} %v_hbm.1, s32[1,32]{1,0:T(1,128)} %lists.1, s32[1]{0:T(128)S(6)} %copy.11.counts), custom_call_target="tpu_custom_call" | custom-call | tf_op jit(solution)/shard_map/pallas_call | solution.py:296
  38.0 0.7 %copy.9 = f32[16,4096]{1,0:T(8,128)} copy(f32[16,4096]{1,0:T(8,128)S(1)} %get-tuple-element.2) | data formatting | bytes 524288
  38.7 0.6 %copy.10 = f32[16,32]{1,0:T(8,128)} copy(f32[16,32]{1,0:T(8,128)S(1)} %get-tuple-element.3) | data formatting | bytes 4096
